TPU v7x, 32 devices: a whole 2x2x4 slice. The times are simulated.
32 devices in a mesh: groups: 2 (over y), seq: 4 (over z), adapter: 2 (over x), head: 2 (over core).
Axes of the slice: x: 2, y: 2, z: 4, core: 2. Of those that a mesh axis runs over, the one named last changes fastest.
Arguments:
- hidden: bfloat16 [64, 3, 8192], P(('groups', 'seq', 'adapter'), None, 'head'), parts along dimension 0, may hold values from -6 to 6
- base_query_rows: bfloat16 [64, 3, 8192], P(('groups', 'seq', 'adapter'), None, 'head'), parts along dimension 0, may hold values from -16 to 16
- fresh_key_value: bfloat16 [2, 64, 3, 1024], P(None, ('groups', 'seq', 'adapter'), None, 'head'), parts along dimension 1, may hold values from -12 to 12
- suffix_key_value: bfloat16 [2, 64, 32, 1024], P(None, ('groups', 'seq', 'adapter'), None, 'head'), parts along dimension 1, may hold values from -12 to 12
- suffix_length: int32 [64], P(('groups', 'seq', 'adapter')), parts along dimension 0, may hold values from 0 to 32, as said below
- row_adapter_index: int32 [64, 1], P(('groups', 'seq', 'adapter')), parts along dimension 0, may hold values from 0 to 1
- prompt_key_value: bfloat16 [2, 8192, 1024], P(None, ('groups', 'seq'), 'head'), parts along dimension 1, may hold values from -16 to 16
- query_down_factors: bfloat16 [4, 64, 8192], P(('groups', 'adapter'), None, 'head'), parts along dimension 0, may hold values from -0.0625 to 0.0625
- query_up_factors: bfloat16 [4, 64, 8192], P(('groups', 'adapter'), None, 'head'), parts along dimension 0, may hold values from -0.75 to 0.75
- output_down_factors: bfloat16 [4, 64, 8192], P(('groups', 'adapter'), None, 'head'), parts along dimension 0, may hold values from -0.0625 to 0.0625
- output_up_factors: bfloat16 [4, 64, 8192], P(('groups', 'adapter'), None, 'head'), parts along dimension 0, may hold values from -0.75 to 0.75
Outputs:
- attended: bfloat16 [64, 3, 8192], P(('groups', 'seq', 'adapter'), None, 'head'), parts along dimension 0
- adapted: bfloat16 [64, 3, 8192], P(('groups', 'seq', 'adapter'), None, 'head'), parts along dimension 0
There are 2 independent parts, one for each index of `groups`. A program takes and returns all parts, laid end to end along the dimension named above; each array names one. Nothing has to cross between parts.
Inputs may be any that keep to these rules, and one draw needn't show every extreme that they name: `suffix_length`: each row's suffix holds at most 32 tokens, and some row holds exactly 32.
All inputs are finite; a program needn't handle non-finite values.
Results may differ from a plain program's by a relative error of at most 0.011.
Values may be sent and summed in bfloat16 or wider, within the bound.
A program may use at most 64 MiB of HBM per device.

v0:
```python
import math

import jax
import jax.numpy as jnp
from jax import lax
from jax.sharding import PartitionSpec as P

HEAD_SIZE = 128


rope_base = 1000000.0


def rotate(values_in, position):
    half_dim = values_in.shape[-1] // 2
    frequency = rope_base ** (-2.0 * jnp.arange(half_dim, dtype=jnp.float32) / values_in.shape[-1])
    angles = position[..., None] * frequency
    cos_part = jnp.cos(angles)
    sin_part = jnp.sin(angles)
    first_half = values_in[..., :half_dim]
    second_half = values_in[..., half_dim:]
    return jnp.concatenate(
        [
            first_half * cos_part - second_half * sin_part,
            second_half * cos_part + first_half * sin_part,
        ],
        -1,
    )


def rank_mask(rank_whole, adapter_of_row, first_adapter, adapter_count):
    picked = (
        adapter_of_row[:, None]
        == first_adapter + jnp.arange(adapter_count, dtype=jnp.int32)[None, :]
    )
    return jnp.where(picked[:, None, :, None], rank_whole, jnp.zeros((), jnp.bfloat16))


def on_device(
    hidden,
    base_query_rows,
    fresh_key_value,
    suffix_key_value,
    suffix_length,
    row_adapter_index,
    prompt_key_value,
    query_down_factors,
    query_up_factors,
    output_down_factors,
    output_up_factors,
):
    row_count = hidden.shape[0]
    step_count = hidden.shape[1]
    head_dim = HEAD_SIZE
    kv_heads = prompt_key_value.shape[2] // head_dim
    query_heads = base_query_rows.shape[2] // head_dim
    group_size = query_heads // kv_heads
    resident_adapters = query_down_factors.shape[0]
    first_adapter = lax.axis_index("adapter") * resident_adapters
    score_scale = 1.0 / math.sqrt(head_dim)
    relocated, moved_ids = (
        lax.all_gather(hidden, "adapter", axis=0, tiled=True),
        lax.all_gather(row_adapter_index, "adapter", axis=0, tiled=True),
    )
    rank_piece = jnp.einsum(
        "mza,uya->mzuy", relocated, query_down_factors, preferred_element_type=jnp.float32
    )
    rank_whole = lax.psum(rank_piece, "head").astype(jnp.bfloat16)
    chosen = rank_mask(rank_whole, moved_ids[:, 0], first_adapter, resident_adapters)
    chosen = chosen.reshape(chosen.shape[0], step_count, -1)
    up_factor_matrix = query_up_factors.reshape(-1, query_up_factors.shape[2])
    picked_rows = chosen
    query_adjustment = lax.psum_scatter(
        jnp.einsum(
            "rtk,kc->rtc", picked_rows, up_factor_matrix, preferred_element_type=jnp.float32
        ),
        "adapter",
        scatter_dimension=0,
        tiled=True,
    )
    prompt_total = prompt_key_value.shape[1] * lax.axis_size("seq")
    position = (
        prompt_total + suffix_length[:, None] + jnp.arange(step_count, dtype=jnp.int32)[None, :]
    ).astype(jnp.float32)
    merged_query = (base_query_rows.astype(jnp.float32) + query_adjustment).reshape(
        row_count, step_count, query_heads, head_dim
    )
    rotated = rotate(merged_query, position[:, :, None]).astype(jnp.bfloat16)
    token_count = row_count * step_count
    query_flat = rotated.reshape(token_count, query_heads * head_dim)
    gathered = lax.all_gather(query_flat, "seq", axis=0, tiled=True)
    seq_count = lax.axis_size("seq")
    block_rows = math.gcd(seq_count, 4) * token_count
    prompt_keys = prompt_key_value[0].reshape(-1, kv_heads, head_dim)
    prompt_values = prompt_key_value[1].reshape(-1, kv_heads, head_dim)

    def prompt_block(block):
        grouped = block.reshape(block_rows, kv_heads, group_size, head_dim)
        scores = (
            jnp.einsum("nkgd,pkd->nkgp", grouped, prompt_keys, preferred_element_type=jnp.float32)
            * score_scale
        )
        peaks = jnp.max(scores, -1)
        weight = jnp.exp(scores - peaks[..., None]).astype(jnp.bfloat16)
        weighted = jnp.einsum(
            "nkgp,pkd->nkgd", weight, prompt_values, preferred_element_type=jnp.float32
        )
        return (weighted, peaks, jnp.sum(weight, -1, dtype=jnp.float32))

    weighted, peaks, totals = lax.map(
        prompt_block, gathered.reshape(-1, block_rows, query_heads * head_dim)
    )
    weighted = weighted.reshape(seq_count, token_count, kv_heads, group_size, head_dim)
    peaks = peaks.reshape(seq_count, token_count, kv_heads, group_size)
    totals = totals.reshape(seq_count, token_count, kv_heads, group_size)
    suffix_slots = suffix_key_value.shape[2]
    local_keys = jnp.concatenate([suffix_key_value[0], fresh_key_value[0]], 1).reshape(
        row_count, suffix_slots + step_count, kv_heads, head_dim
    )
    local_values = jnp.concatenate([suffix_key_value[1], fresh_key_value[1]], 1).reshape(
        row_count, suffix_slots + step_count, kv_heads, head_dim
    )
    own_query = rotated.reshape(row_count, step_count, kv_heads, group_size, head_dim)
    local_scores = (
        jnp.einsum("rtkgd,rpkd->rtkgp", own_query, local_keys, preferred_element_type=jnp.float32)
        * score_scale
    )
    key_slot = jnp.arange(suffix_slots + step_count, dtype=jnp.int32)[None, None, :]
    admitted = jnp.where(
        key_slot < suffix_slots,
        key_slot < suffix_length[:, None, None],
        key_slot - suffix_slots <= jnp.arange(step_count, dtype=jnp.int32)[None, :, None],
    )
    admitted = admitted[:, :, None, None, :]
    masked = jnp.where(admitted, local_scores, -1e30)
    local_peaks = jnp.max(masked, -1)
    local_weight = jnp.where(admitted, jnp.exp(masked - local_peaks[..., None]), 0.0).astype(
        jnp.bfloat16
    )
    local_weighted = jnp.einsum(
        "rtkgp,rpkd->rtkgd", local_weight, local_values, preferred_element_type=jnp.float32
    )
    local_totals = jnp.sum(local_weight, -1, dtype=jnp.float32)
    local_part = (
        local_weighted.reshape(token_count, kv_heads, group_size, head_dim),
        local_peaks.reshape(token_count, kv_heads, group_size),
        local_totals.reshape(token_count, kv_heads, group_size),
    )
    arrived = (
        lax.all_to_all(weighted, "seq", split_axis=0, concat_axis=0, tiled=True),
        lax.all_to_all(peaks, "seq", split_axis=0, concat_axis=0, tiled=True),
        lax.all_to_all(totals, "seq", split_axis=0, concat_axis=0, tiled=True),
    )
    highest = jnp.maximum(jnp.max(arrived[1], 0), local_part[1])
    factors = jnp.exp(arrived[1] - highest[None])
    local_factor = jnp.exp(local_part[1] - highest)
    combined = (
        jnp.sum(arrived[0] * factors[..., None], 0) + local_part[0] * local_factor[..., None],
        highest,
        jnp.sum(arrived[2] * factors, 0) + local_part[2] * local_factor,
    )
    attended = (
        (combined[0] / combined[2][..., None])
        .reshape(row_count, step_count, query_heads * head_dim)
        .astype(jnp.bfloat16)
    )
    relocated_output = lax.all_gather(attended, "adapter", axis=0, tiled=True)
    out_adapter = moved_ids[:, 0]
    output_piece = jnp.einsum(
        "aod,bxd->aobx", relocated_output, output_down_factors, preferred_element_type=jnp.float32
    )
    out_whole = lax.psum(output_piece, "head").astype(jnp.bfloat16)
    out_chosen = rank_mask(out_whole, out_adapter, first_adapter, resident_adapters)
    out_chosen = out_chosen.reshape(out_chosen.shape[0], step_count, -1)
    output_matrix = output_up_factors.reshape(-1, output_up_factors.shape[2])
    picked_rows = out_chosen
    adapted = lax.psum_scatter(
        jnp.einsum(
            "rtk,kc->rtc", picked_rows, output_matrix, preferred_element_type=jnp.float32
        ).astype(jnp.bfloat16),
        "adapter",
        scatter_dimension=0,
        tiled=True,
    )
    return (attended, adapted)


def solution(mesh):
    placed = (
        P(("groups", "seq", "adapter"), None, "head"),
        P(("groups", "seq", "adapter"), None, "head"),
        P(None, ("groups", "seq", "adapter"), None, "head"),
        P(None, ("groups", "seq", "adapter"), None, "head"),
        P(("groups", "seq", "adapter")),
        P(("groups", "seq", "adapter"), None),
        P(None, ("groups", "seq"), "head"),
        P(("groups", "adapter"), None, "head"),
        P(("groups", "adapter"), None, "head"),
        P(("groups", "adapter"), None, "head"),
        P(("groups", "adapter"), None, "head"),
    )
    return jax.shard_map(
        on_device,
        mesh=mesh,
        in_specs=placed,
        out_specs=(
            P(("groups", "seq", "adapter"), None, "head"),
            P(("groups", "seq", "adapter"), None, "head"),
        ),
        check_vma=False,
    )
```

profile of v0, /device:TPU:0, one launch (start us, length us, event | category | flops | bytes accessed | tf_op | source)
XLA Modules:
  0.0 158.0 jit_solution(6702682194150986861)
XLA Ops:
  7.3 1.3 fusion.39
  10.0 5.2 %all-reduce = s32[8]{0:T(128)S(1)} all-reduce(s32[8]{0:T(128)S(1)} %bitcast_dynamic-update-slice_fusion), channel_id=1, replica_groups=mesh['groups'=2,'seq'=4,'adapter'=2,'head'=2] {'adapter'}, use_global_device_ids=true, to_apply=%add | all-reduce | flops 8 | bytes 64
  16.2 5.6 %all_gather.13 = bf16[8,3,4096]{2,1,0:T(4,128)(2,1)S(1)} all-gather(bf16[4,3,4096]{2,1,0:T(4,128)(2,1)S(1)} %copy.71), channel_id=1, replica_groups=mesh['groups'=2,'seq'=4,'adapter'=2,'head'=2] {'adapter'}, dimensions={0}, use_global_device_ids=true | all-gather | bytes 294912 | tf_op jit(solution)/shard_map/all_gather | solution.py:62
  21.8 1.4 convolution_bitcast_fusion.2
  23.2 3.3 %psum.14 = bf16[8,3,1,64]{3,0,1,2:T(8,128)(2,1)S(1)} all-reduce(f32[8,3,1,64]{3,0,1,2:T(8,128)S(1)} %convolution_bitcast_fusion.2), channel_id=1, replica_groups=mesh['groups'=2,'seq'=4,'adapter'=2,'head'=2] {'head'}, use_global_device_ids=true, to_apply=%region_0.0 | all-reduce | flops 1536 | bytes 9216 | tf_op jit(solution)/shard_map/psum | solution.py:68
  27.5 1.3 iota_compare_fusion.1
  29.5 1.3 fusion.38
  30.8 2.7 %fusion.36 = (bf16[1,1024,512]{2,1,0:T(8,128)(2,1)S(1)}, bf16[1,1024,512]{2,1,0:T(8,128)(2,1)}) fusion(bf16[2,1024,512]{2,1,0:T(8,128)(2,1)} %param.17), kind=kLoop, calls=%fused_computation.71 | loop fusion | bytes 4194304 | tf_op jit(solution)/shard_map/slice | solution.py:95
  33.5 1.5 copy.130
  37.0 18.2 %all-reduce.6.cloned.1.call-done = f32[8,3,4096]{2,0,1:T(8,128)} async-done(((f32[8,3,4096]{2,0,1:T(8,128)}), f32[8,3,4096]{2,0,1:T(8,128)}) %all-reduce.6.cloned.1.call-update) | async-done | bytes 393232
  57.4 15.5 %all-gather = bf16[4,12,4096]{2,1,0:T(8,128)(2,1)S(1)} all-gather(bf16[1,12,4096]{2,1,0:T(8,128)(2,1)S(1)} %reshape.233), channel_id=1, replica_groups=mesh['groups'=2,'seq'=4,'adapter'=2,'head'=2] {'seq'}, dimensions={0}, use_global_device_ids=true | all-gather | bytes 491520 | tf_op jit(solution)/shard_map/all_gather | solution.py:91
  74.3 2.7 %copy-done.1 = f32[4,48,8,1024]{3,2,1,0:T(8,128)} copy-done((f32[4,48,8,1024]{3,2,1,0:T(8,128)}, f32[4,48,8,1024]{3,2,1,0:T(8,128)S(1)}, u32[]{:S(2)}) %copy-start.1) | copy-done | bytes 6291480
  76.9 1.3 convert_reduce_fusion
  79.2 5.4 %all-to-all-start.2 = ((f32[4,1,384]{2,1,0:T(1,128)}), f32[4,1,384]{2,1,0:T(1,128)S(1)}, u32[]{:S(2)}, u32[]{:S(2)}) async-start(f32[4,1,384]{2,1,0:T(1,128)} %reshape.257), calls=%async_computation.2 | async-start | bytes 12288 | tf_op jit(solution)/shard_map/all_to_all | solution.py:152
  86.0 4.1 %all-to-all-done.2 = f32[4,1,384]{2,1,0:T(1,128)S(1)} async-done(((f32[4,1,384]{2,1,0:T(1,128)}), f32[4,1,384]{2,1,0:T(1,128)S(1)}, u32[]{:S(2)}, u32[]{:S(2)}) %all-to-all-start.2) | async-done | bytes 6176 | tf_op jit(solution)/shard_map/all_to_all | solution.py:152
  90.1 3.2 %all-to-all-start.1 = ((f32[4,1,384]{2,1,0:T(1,128)}), f32[4,1,384]{2,1,0:T(1,128)S(1)}, u32[]{:S(2)}, u32[]{:S(2)}) async-start(f32[4,1,384]{2,1,0:T(1,128)} %reshape.259), calls=%async_computation.1 | async-start | bytes 12288 | tf_op jit(solution)/shard_map/all_to_all | solution.py:151
  93.4 4.0 %fusion.9 = f32[4,48,8,128]{3,2,1,0:T(8,128)S(1)} fusion(bf16[1024,4,128,1]{0,2,3,1:T(8,128)(2,1)S(1)} %bitcast.113, f32[4,48,8,1024]{3,2,1,0:T(8,128)} %copy-done.1, f32[48,4,8]{2,0,1:T(8,128)S(1)} %get-tuple-element.43), kind=kOutput, calls=%fused_computation.18 | convolution fusion | flops 407371776 | bytes 8132608 | tf_op jit(solution)/shard_map/while/body/eval_jaxpr/nkgp,pkd->nkgd/dot_general | solution.py:105
  98.9 4.6 %all-to-all-start = ((f32[4,12,4,8,128]{4,3,1,2,0:T(8,128)}), f32[4,12,4,8,128]{4,3,1,2,0:T(8,128)S(1)}, u32[]{:S(2)}, u32[]{:S(2)}) async-start(f32[4,12,4,8,128]{4,3,1,2,0:T(8,128)} %copy.79), calls=%async_computation | async-start | bytes 1572864 | tf_op jit(solution)/shard_map/all_to_all | solution.py:150
  104.7 1.3 fusion.40
  109.8 8.4 %all-to-all-done = f32[4,12,4,8,128]{4,3,1,2,0:T(8,128)S(1)} async-done(((f32[4,12,4,8,128]{4,3,1,2,0:T(8,128)}), f32[4,12,4,8,128]{4,3,1,2,0:T(8,128)S(1)}, u32[]{:S(2)}, u32[]{:S(2)}) %all-to-all-start) | async-done | bytes 786464 | tf_op jit(solution)/shard_map/all_to_all | solution.py:150
  118.7 5.6 %all_gather.15 = bf16[8,3,4096]{2,1,0:T(4,128)(2,1)S(1)} all-gather(bf16[4,3,4096]{2,1,0:T(4,128)(2,1)S(1)} %fusion.13), channel_id=1, replica_groups=mesh['groups'=2,'seq'=4,'adapter'=2,'head'=2] {'adapter'}, dimensions={0}, use_global_device_ids=true | all-gather | bytes 294912 | tf_op jit(solution)/shard_map/all_gather | solution.py:167
  124.7 3.3 %psum.15 = bf16[8,3,1,64]{3,0,1,2:T(8,128)(2,1)S(1)} all-reduce(f32[8,3,1,64]{3,0,1,2:T(8,128)S(1)} %convolution_bitcast_fusion.1), channel_id=1, replica_groups=mesh['groups'=2,'seq'=4,'adapter'=2,'head'=2] {'head'}, use_global_device_ids=true, to_apply=%region_9.10 | all-reduce | flops 1536 | bytes 9216 | tf_op jit(solution)/shard_map/psum | solution.py:172
  129.7 19.9 %all-reduce.8.cloned.1.call-done = bf16[8,3,4096]{2,0,1:T(8,128)(2,1)} async-done(((bf16[8,3,4096]{2,0,1:T(8,128)(2,1)}), bf16[8,3,4096]{2,0,1:T(8,128)(2,1)}) %all-reduce.8.cloned.1.call-update) | async-done | bytes 196624
  149.6 1.6 %constant_dynamic-slice_fusion = bf16[4,3,4096]{2,0,1:T(4,128)(2,1)} fusion(bf16[8,3,4096]{2,0,1:T(8,128)(2,1)} %all-reduce.8.cloned.1.call-done, u32[]{:T(128)S(6)} %multiply.11), kind=kLoop, calls=%fused_computation.59 | loop fusion | bytes 196612
  (99 shorter events, 19.4 us)
Async XLA Ops:
  7.2 19.3 %copy-start = (bf16[1,64,4096]{2,1,0:T(8,128)(2,1)S(1)}, bf16[1,64,4096]{2,1,0:T(8,128)(2,1)}, u32[]{:S(2)}) copy-start(bf16[1,64,4096]{2,1,0:T(8,128)(2,1)} %param.19) | copy-start | bytes 1572868
  7.2 29.1 %copy-start.7 = (bf16[2,4,32,512]{3,2,1,0:T(8,128)(2,1)S(1)}, bf16[2,4,32,512]{3,2,1,0:T(8,128)(2,1)}, u32[]{:S(2)}) copy-start(bf16[2,4,32,512]{3,2,1,0:T(8,128)(2,1)} %param.14) | copy-start | bytes 786436
  7.2 48.1 %copy-start.8 = (bf16[4,3,4096]{2,0,1:T(4,128)(2,1)S(1)}, bf16[4,3,4096]{2,0,1:T(4,128)(2,1)}, u32[]{:S(2)}) copy-start(bf16[4,3,4096]{2,0,1:T(4,128)(2,1)} %param.12) | copy-start | bytes 294916
  7.2 48.1 %all-reduce.6.cloned.1.call-start = ((), (), s32[]{:S(2)}) async-start(), calls=%async_computation.3 | async-start | bytes 786432
  56.6 0.6 copy-start.5
  56.6 0.7 copy-start.6
  74.2 2.7 %copy-start.1 = (f32[4,48,8,1024]{3,2,1,0:T(8,128)}, f32[4,48,8,1024]{3,2,1,0:T(8,128)S(1)}, u32[]{:S(2)}) copy-start(f32[4,48,8,1024]{3,2,1,0:T(8,128)S(1)} %get-tuple-element.44) | copy-start | bytes 18874372
  79.2 11.0 %all-to-all-start.2 = ((f32[4,1,384]{2,1,0:T(1,128)}), f32[4,1,384]{2,1,0:T(1,128)S(1)}, u32[]{:S(2)}, u32[]{:S(2)}) async-start(f32[4,1,384]{2,1,0:T(1,128)} %reshape.257), calls=%async_computation.2 | async-start | bytes 12288 | tf_op jit(solution)/shard_map/all_to_all | solution.py:152
  85.1 18.4 %copy-start.10 = (pred[4,35]{1,0:T(4,128)(4,1)S(1)}, pred[4,35]{1,0:T(4,128)(4,1)}, u32[]{:S(2)}) copy-start(pred[4,35]{1,0:T(4,128)(4,1)} %iota_compare_fusion.1) | copy-start | bytes 424
  85.1 18.4 %copy-start.11 = (pred[3,35]{1,0:T(4,128)(4,1)S(1)}, pred[3,35]{1,0:T(4,128)(4,1)}, u32[]{:S(2)}) copy-start(pred[3,35]{1,0:T(4,128)(4,1)} %iota_compare_fusion) | copy-start | bytes 319
  85.1 18.4 %copy-start.9 = (bf16[1,4,3,512]{3,1,2,0:T(4,128)(2,1)S(1)}, bf16[1,4,3,512]{3,1,2,0:T(4,128)(2,1)}, u32[]{:S(2)}) copy-start(bf16[1,4,3,512]{3,1,2,0:T(4,128)(2,1)} %get-tuple-element.37) | copy-start | bytes 36868
  85.1 19.5 %copy-start.4 = (bf16[1,4,32,512]{3,2,1,0:T(8,128)(2,1)S(1)}, bf16[1,4,32,512]{3,2,1,0:T(8,128)(2,1)}, u32[]{:S(2)}) copy-start(bf16[1,4,32,512]{3,2,1,0:T(8,128)(2,1)} %get-tuple-element.34) | copy-start | bytes 393220
  90.1 8.8 %all-to-all-start.1 = ((f32[4,1,384]{2,1,0:T(1,128)}), f32[4,1,384]{2,1,0:T(1,128)S(1)}, u32[]{:S(2)}, u32[]{:S(2)}) async-start(f32[4,1,384]{2,1,0:T(1,128)} %reshape.259), calls=%async_computation.1 | async-start | bytes 12288 | tf_op jit(solution)/shard_map/all_to_all | solution.py:151
  97.4 27.0 %copy-start.3 = (bf16[1,64,4096]{2,1,0:T(8,128)(2,1)S(1)}, bf16[1,64,4096]{2,1,0:T(8,128)(2,1)}, u32[]{:S(2)}) copy-start(bf16[1,64,4096]{2,1,0:T(8,128)(2,1)} %param.20) | copy-start | bytes 1572868
  98.3 29.6 %copy-start.2 = (bf16[1,64,4096]{2,1,0:T(8,128)(2,1)S(1)}, bf16[1,64,4096]{2,1,0:T(8,128)(2,1)}, u32[]{:S(2)}) copy-start(bf16[1,64,4096]{2,1,0:T(8,128)(2,1)} %param.21) | copy-start | bytes 1572868
  98.9 19.3 %all-to-all-start = ((f32[4,12,4,8,128]{4,3,1,2,0:T(8,128)}), f32[4,12,4,8,128]{4,3,1,2,0:T(8,128)S(1)}, u32[]{:S(2)}, u32[]{:S(2)}) async-start(f32[4,12,4,8,128]{4,3,1,2,0:T(8,128)} %copy.79), calls=%async_computation | async-start | bytes 1572864 | tf_op jit(solution)/shard_map/all_to_all | solution.py:150
  103.5 46.0 %all-reduce.8.cloned.1.call-start = ((), (), s32[]{:S(2)}) async-start(), calls=%async_computation.4 | async-start | bytes 393216
Sparse Core Ops, SparseCore 0:
  27.7 27.5 all-reduce.5
  129.1 20.4 all-reduce.7
where the time goes:
time: 159 us; the launch traced here: 158 us
  waiting for transfers between devices  51.2 us (32%)
  blocking collectives  38.6 us (24%)
  local copies, waits for them, and re-layouts  21.6 us (14%)
  between operations  15.8 us (10%)
  starting transfers between devices  13.3 us (8%)
  matrix products  10.3 us (6%)
  other arithmetic  7.28 us (5%)
    unnamed x4, waiting for transfers between devices  38.2 us
    all_gather x1, blocking collectives, on_device(): gathered = lax.all_gather(query_flat, 'seq', axis=0, tiled=True)  15.5 us
    unnamed x37, local copies, waits for them, and re-layouts  12.4 us
    all_to_all x1, waiting for transfers between devices, on_device(): lax.all_to_all(weighted, 'seq', split_axis=0, concat_axis=0, tiled=True)  8.4 us
    all_gather x1, blocking collectives, on_device(): lax.all_gather(hidden, 'adapter', axis=0, tiled=True)  5.64 us
    all_gather x1, blocking collectives, on_device(): relocated_output = lax.all_gather(attended, 'adapter', axis=0, tiled=True)  5.64 us
    all_to_all x1, starting transfers between devices, on_device(): lax.all_to_all(totals, 'seq', split_axis=0, concat_axis=0, tiled=True)  5.38 us
    unnamed x1, blocking collectives  5.22 us
  transfers between devices with their start and end apart: 5, of which 5 were waited for; matrix products, arithmetic and copies ran while one was open for 14% of the time, Pallas kernels for 0%

commit v1 on v0

v1 whole, which is shorter than its diff:
```python
import functools
import math

import jax
import jax.numpy as jnp
import numpy as np
from jax import lax
from jax.experimental import pallas as pl
from jax.experimental.pallas import tpu as pltpu
from jax.sharding import PartitionSpec as P

HEAD_SIZE = 128
ROPE_BASE = 1000000.0
MESH = pl.DeviceIdType.MESH
NT = (((1,), (1,)), ((), ()))


def dot_nt(a, b):
    return lax.dot_general(a, b, NT, preferred_element_type=jnp.float32)


def dot_nn(a, b):
    return jnp.dot(a, b, preferred_element_type=jnp.float32)


def body(
    cfg,
    len_ref,
    id_ref,
    cos_ref,
    sin_ref,
    hidden_hbm,
    base_hbm,
    fresh_hbm,
    suffix_hbm,
    prompt_hbm,
    qd_hbm,
    qu_hbm,
    od_hbm,
    ou_hbm,
    att_ref,
    ada_ref,
    hidden_v,
    base_v,
    fresh_v,
    suffix_v,
    prompt_v,
    qd_v,
    qu_v,
    od_v,
    ou_v,
    local_sem,
    hid_in,
    tok_f32,
    rows_f32,
    fresh_pad,
    fresh_f32,
    rk_out,
    rk_in,
    ork_out,
    ork_in,
    dl_out,
    dl_in,
    q_own,
    q_in,
    part_out,
    part_in,
    stat_out,
    stat_in,
    own_o,
    own_m,
    own_t,
    at_out,
    at_in,
    ad_out,
    ad_in,
    hid_s,
    hid_r,
    rk_s,
    rk_r,
    ork_s,
    ork_r,
    dl_s,
    dl_r,
    q_s,
    q_r,
    part_s,
    part_r,
    stat_s,
    stat_r,
    at_s,
    at_r,
    ad_s,
    ad_r,
):
    NS, NA, NH, R, T, KV, G, S = cfg
    D = HEAD_SIZE
    N = R * T
    NG = N * G
    C = G * D
    seq, ada, head = lax.axis_index("seq"), lax.axis_index("adapter"), lax.axis_index("head")
    scale = math.log2(math.e) / math.sqrt(D)

    def at_axis(axis, me, offset, size):
        return {axis: lax.rem(me + offset, size)}

    partners = (
        [at_axis("adapter", ada, d, NA) for d in range(1, NA)]
        + [at_axis("head", head, d, NH) for d in range(1, NH)]
        + [at_axis("seq", seq, d, NS) for d in range(1, NS)]
    )
    barrier = pltpu.get_barrier_semaphore()
    for partner in partners:
        pl.semaphore_signal(barrier, inc=1, device_id=partner, device_id_type=MESH)

    loads = []
    for i, (src, dst) in enumerate(
        (
            (hidden_hbm, hidden_v),
            (qd_hbm, qd_v),
            (qu_hbm, qu_v),
            (base_hbm, base_v),
            (prompt_hbm, prompt_v),
            (suffix_hbm, suffix_v),
            (fresh_hbm, fresh_v),
            (od_hbm, od_v),
            (ou_hbm, ou_v),
        )
    ):
        load = pltpu.make_async_copy(src, dst, local_sem.at[i])
        load.start()
        loads.append(load)
    l_hid, l_qd, l_qu, l_base, l_prompt, l_suffix, l_fresh, l_od, l_ou = loads

    pl.semaphore_wait(barrier, len(partners))

    sends = []

    def send(src, dst, s_sem, r_sem, device):
        copy = pltpu.make_async_remote_copy(
            src_ref=src,
            dst_ref=dst,
            send_sem=s_sem,
            recv_sem=r_sem,
            device_id=device,
            device_id_type=MESH,
        )
        copy.start()
        sends.append(copy)
        return copy

    hid = {}
    for d in range(1, NA):
        hid[d] = send(
            hidden_hbm, hid_in.at[d - 1], hid_s.at[d - 1], hid_r.at[d - 1],
            at_axis("adapter", ada, d, NA),
        )

    def gather_tokens(ref):
        for r in range(R):
            tok_f32[r * T : (r + 1) * T, :] = ref[r].astype(jnp.float32)
        return tok_f32[...].astype(jnp.bfloat16)

    rk = {}

    def rank_part(tokens, factors, slot, out_ref, in_ref, s_sem, r_sem):
        out_ref[slot] = dot_nt(tokens, factors)
        send_rank(slot, out_ref, in_ref, s_sem, r_sem)

    def send_rank(slot, out_ref, in_ref, s_sem, r_sem):
        for j in range(1, NH):
            rk[(slot, j)] = send(
                out_ref.at[slot], in_ref.at[j - 1, slot], s_sem.at[j - 1, slot],
                r_sem.at[j - 1, slot], at_axis("head", head, j, NH),
            )

    def rank_whole(slot, out_ref, in_ref):
        total = out_ref[slot]
        for j in range(1, NH):
            rk[(slot, j)].wait_recv()
            total = total + in_ref[j - 1, slot]
        return total.astype(jnp.bfloat16)

    l_hid.wait()
    l_qd.wait()
    rank_part(gather_tokens(hidden_v), qd_v[0], 0, rk_out, rk_in, rk_s, rk_r)
    for d in range(1, NA):
        hid[d].wait_recv()
        rank_part(gather_tokens(hid_in.at[d - 1]), qd_v[0], d, rk_out, rk_in, rk_s, rk_r)

    def to_rows(x):
        for g in range(G):
            rows_f32[pl.ds(g, N, stride=G), :] = x[:, g * D : (g + 1) * D]
        return rows_f32[...]

    def from_rows(x):
        rows_f32[...] = x
        return jnp.concatenate([rows_f32[pl.ds(g, N, stride=G), :] for g in range(G)], 1)

    def put_out(ref, x, k):
        rows_f32[...] = x
        for r in range(R):
            ref[r, :, k * C : (k + 1) * C] = jnp.concatenate(
                [rows_f32[pl.ds(r * T * G + g, T, stride=G), :] for g in range(G)], 1
            ).astype(jnp.bfloat16)

    l_fresh.wait()
    fresh_pad[...] = jnp.zeros_like(fresh_pad)
    for i in range(2):
        fresh_f32[...] = jnp.zeros_like(fresh_f32)
        for r in range(R):
            fresh_f32[r * T : (r + 1) * T, :] = fresh_v[i, r].astype(jnp.float32)
        fresh_pad[i, 0 : fresh_f32.shape[0], :] = fresh_f32[...].astype(jnp.bfloat16)

    l_qu.wait()
    dl = {}
    for d in range(1, NA):
        rank = rank_whole(d, rk_out, rk_in)
        for k in range(KV):
            dl_out[d - 1, k] = to_rows(
                dot_nn(rank, qu_v[0, :, k * C : (k + 1) * C])
            ).astype(jnp.bfloat16)
            dl[(d, k)] = send(
                dl_out.at[d - 1, k], dl_in.at[d - 1, k], dl_s.at[d - 1, k],
                dl_r.at[d - 1, k], at_axis("adapter", ada, NA - d, NA),
            )
    row_of = lax.broadcasted_iota(jnp.int32, (NG, D), 0)
    lane = lax.broadcasted_iota(jnp.int32, (NG, D), 1)
    eye = row_of == lane
    row_index = row_of // (T * G)
    ids = jnp.zeros((NG, D), jnp.int32)
    lengths = jnp.zeros((NG, D), jnp.int32)
    for r in range(R):
        ids = jnp.where(row_index == r, id_ref[r, 0], ids)
        lengths = jnp.where(row_index == r, len_ref[r], lengths)
    step_of = (row_of - row_index * (T * G)) // G

    def pick(own, ref, k):
        out = own
        for d in range(1, NA):
            out = jnp.where(
                ids == lax.rem(ada + d, NA), ref[d - 1, k].astype(jnp.float32), out
            )
        return out

    cos = jnp.concatenate(
        [jnp.broadcast_to(cos_ref[pl.ds(len_ref[n // T] + n % T, 1), :], (G, D)) for n in range(N)], 0
    )
    sin = jnp.concatenate(
        [jnp.broadcast_to(sin_ref[pl.ds(len_ref[n // T] + n % T, 1), :], (G, D)) for n in range(N)], 0
    )

    rank = rank_whole(0, rk_out, rk_in)
    l_base.wait()
    qs = {}
    order = sorted(range(1, NS), key=lambda d: (min(d, NS - d), d))
    for k in range(KV):
        delta = to_rows(dot_nn(rank, qu_v[0, :, k * C : (k + 1) * C]))
        for r in range(R):
            x = base_v[r, :, k * C : (k + 1) * C].astype(jnp.float32)
            for g in range(G):
                rows_f32[pl.ds(r * T * G + g, T, stride=G), :] = x[:, g * D : (g + 1) * D]
        base = rows_f32[...]
        for d in range(1, NA):
            dl[(d, k)].wait_recv()
        merged = base + pick(delta, dl_in, k)
        turned = merged * cos + pltpu.roll(merged, D // 2, 1) * sin
        q_own[k] = turned.astype(jnp.bfloat16)
        for d in order:
            qs[(d, k)] = send(
                q_own.at[k], q_in.at[d - 1, k], q_s.at[d - 1, k], q_r.at[d - 1, k],
                at_axis("seq", seq, d, NS),
            )

    l_prompt.wait()
    l_suffix.wait()

    def values_of(v):
        return jnp.concatenate([v, jnp.ones((v.shape[0], D), jnp.bfloat16)], 1)

    def prompt_part(query, k):
        cols = slice(k * D, (k + 1) * D)
        scores = dot_nt(query, prompt_v[0, :, cols])
        peak = jnp.max(scores, -1, keepdims=True)
        weight = jnp.exp2((scores - peak) * scale).astype(jnp.bfloat16)
        both = dot_nn(weight, values_of(prompt_v[1, :, cols]))
        return both[:, :D], peak, both[:, D:]

    def local_part(query, k):
        cols = slice(k * D, (k + 1) * D)
        n_suf = R * S
        s_keys = suffix_v[0, :, :, cols].reshape(n_suf, D)
        s_vals = suffix_v[1, :, :, cols].reshape(n_suf, D)
        scores = jnp.concatenate(
            [dot_nt(query, s_keys), dot_nt(query, fresh_pad[0, :, cols])], 1
        )
        masked = jnp.where(admitted, scores, -1e30)
        peak = jnp.max(masked, -1, keepdims=True)
        weight = jnp.where(admitted, jnp.exp2((masked - peak) * scale), 0.0).astype(jnp.bfloat16)
        both = dot_nn(
            weight, values_of(jnp.concatenate([s_vals, fresh_pad[1, :, cols]], 0))
        )
        return both[:, :D], peak, both[:, D:]

    n_suf = R * S
    s_row = lax.broadcasted_iota(jnp.int32, (NG, n_suf), 0) // (T * G)
    s_col = lax.broadcasted_iota(jnp.int32, (NG, n_suf), 1)
    s_len = jnp.concatenate([lengths] * (n_suf // D), 1)
    in_suffix = (s_col // S == s_row) & (s_col - s_row * S < s_len)
    f_slot = lane - row_index * T
    in_fresh = (f_slot >= 0) & (f_slot <= step_of)
    admitted = jnp.concatenate(
        [in_suffix.astype(jnp.int32), in_fresh.astype(jnp.int32)], 1
    ) != 0

    def merge(parts):
        top = functools.reduce(jnp.maximum, [p[1] for p in parts])
        factors = [jnp.exp2((p[1] - top) * scale) for p in parts]
        num = functools.reduce(jnp.add, [p[0] * f for p, f in zip(parts, factors)])
        den = functools.reduce(jnp.add, [p[2] * f for p, f in zip(parts, factors)])
        return num, top, den

    for k in range(KV):
        query = q_own[k]
        o, m, t = merge([prompt_part(query, k), local_part(query, k)])
        own_o[k] = o
        own_m[k] = jnp.broadcast_to(m, (NG, D))
        own_t[k] = t

    parts, stats = {}, {}

    def remote_parts(k):
        for d in order:
            qs[(d, k)].wait_recv()
            o, m, t = prompt_part(q_in[d - 1, k], k)
            part_out[d - 1, k] = o.astype(jnp.bfloat16)
            stat_out[d - 1, k, 0:1, 0:D] = jnp.sum(jnp.where(eye, m, 0.0), 0, keepdims=True)
            stat_out[d - 1, k, 1:2, 0:D] = jnp.sum(jnp.where(eye, t, 0.0), 0, keepdims=True)
            home = at_axis("seq", seq, NS - d, NS)
            parts[(d, k)] = send(
                part_out.at[d - 1, k], part_in.at[d - 1, k], part_s.at[d - 1, k],
                part_r.at[d - 1, k], home,
            )
            stats[(d, k)] = send(
                stat_out.at[d - 1, k], stat_in.at[d - 1, k], stat_s.at[d - 1, k],
                stat_r.at[d - 1, k], home,
            )

    at = {}
    own_rank = [jnp.zeros((N, od_v.shape[1]), jnp.float32)]

    def column(row):
        return jnp.sum(jnp.where(eye, row, 0.0), 1, keepdims=True)

    def combine(k):
        pieces = [(own_o[k], own_m[k], own_t[k])]
        for d in order:
            parts[(d, k)].wait_recv()
            stats[(d, k)].wait_recv()
            pieces.append(
                (
                    part_in[d - 1, k].astype(jnp.float32),
                    column(stat_in[d - 1, k, 0:1, :]),
                    column(stat_in[d - 1, k, 1:2, :]),
                )
            )
        num, top, den = merge(pieces)
        result = (num / den).astype(jnp.bfloat16)
        at_out[k] = result
        for d in range(1, NA):
            at[(d, k)] = send(
                at_out.at[k], at_in.at[d - 1, k], at_s.at[d - 1, k], at_r.at[d - 1, k],
                at_axis("adapter", ada, d, NA),
            )
        wide = result.astype(jnp.float32)
        put_out(att_ref, wide, k)
        own_rank[0] = own_rank[0] + dot_nt(
            from_rows(wide).astype(jnp.bfloat16), od_v[0, :, k * C : (k + 1) * C]
        )

    for k in range(KV):
        remote_parts(k)
        if k == 0:
            l_od.wait()
        if k > 0:
            combine(k - 1)
    combine(KV - 1)

    rk = {}
    ork_out[0] = own_rank[0]
    send_rank(0, ork_out, ork_in, ork_s, ork_r)
    for d in range(1, NA):
        acc = jnp.zeros((N, od_v.shape[1]), jnp.float32)
        for k in range(KV):
            at[(d, k)].wait_recv()
            acc = acc + dot_nt(
                from_rows(at_in[d - 1, k].astype(jnp.float32)).astype(jnp.bfloat16),
                od_v[0, :, k * C : (k + 1) * C],
            )
        ork_out[d] = acc
        send_rank(d, ork_out, ork_in, ork_s, ork_r)

    l_ou.wait()
    ad = {}
    for d in range(1, NA):
        rank = rank_whole(d, ork_out, ork_in)
        for k in range(KV):
            ad_out[d - 1, k] = to_rows(
                dot_nn(rank, ou_v[0, :, k * C : (k + 1) * C])
            ).astype(jnp.bfloat16)
            ad[(d, k)] = send(
                ad_out.at[d - 1, k], ad_in.at[d - 1, k], ad_s.at[d - 1, k],
                ad_r.at[d - 1, k], at_axis("adapter", ada, NA - d, NA),
            )
    rank = rank_whole(0, ork_out, ork_in)
    for k in range(KV):
        own = to_rows(dot_nn(rank, ou_v[0, :, k * C : (k + 1) * C]))
        for d in range(1, NA):
            ad[(d, k)].wait_recv()
        put_out(ada_ref, pick(own, ad_in, k), k)

    for copy in sends:
        copy.wait_send()


def on_device(
    hidden,
    base_query_rows,
    fresh_key_value,
    suffix_key_value,
    suffix_length,
    row_adapter_index,
    prompt_key_value,
    query_down_factors,
    query_up_factors,
    output_down_factors,
    output_up_factors,
):
    NS, NA, NH = lax.axis_size("seq"), lax.axis_size("adapter"), lax.axis_size("head")
    R, T, width = hidden.shape
    D = HEAD_SIZE
    KV = prompt_key_value.shape[2] // D
    G = width // D // KV
    S = suffix_key_value.shape[2]
    N, NG = R * T, R * T * G
    rank = query_down_factors.shape[1]
    assert query_down_factors.shape[0] == 1
    prompt_total = prompt_key_value.shape[1] * NS
    positions = prompt_total + np.arange(S + T, dtype=np.float64)
    frequency = ROPE_BASE ** (-2.0 * np.arange(D // 2, dtype=np.float64) / D)
    angle = positions[:, None] * frequency[None, :]
    cos = np.concatenate([np.cos(angle), np.cos(angle)], 1).astype(np.float32)
    sin = np.concatenate([-np.sin(angle), np.sin(angle)], 1).astype(np.float32)
    bf16, f32 = jnp.bfloat16, jnp.float32
    dma = pltpu.SemaphoreType.DMA
    one = max(NA - 1, 1)
    far = max(NS - 1, 1)
    two = max(NH - 1, 1)

    def like(x):
        return pltpu.VMEM(x.shape, x.dtype)

    scratch = [
        like(hidden),
        like(base_query_rows),
        like(fresh_key_value),
        like(suffix_key_value),
        like(prompt_key_value),
        like(query_down_factors),
        like(query_up_factors),
        like(output_down_factors),
        like(output_up_factors),
        dma((9,)),
        pltpu.VMEM((one,) + hidden.shape, bf16),
        pltpu.VMEM((N, width), f32),
        pltpu.VMEM((NG, D), f32),
        pltpu.VMEM((2, D, KV * D), bf16),
        pltpu.VMEM((-(-N // 16) * 16, KV * D), f32),
        pltpu.VMEM((NA, N, rank), f32),
        pltpu.VMEM((two, NA, N, rank), f32),
        pltpu.VMEM((NA, N, rank), f32),
        pltpu.VMEM((two, NA, N, rank), f32),
        pltpu.VMEM((one, KV, NG, D), bf16),
        pltpu.VMEM((one, KV, NG, D), bf16),
        pltpu.VMEM((KV, NG, D), bf16),
        pltpu.VMEM((far, KV, NG, D), bf16),
        pltpu.VMEM((far, KV, NG, D), bf16),
        pltpu.VMEM((far, KV, NG, D), bf16),
        pltpu.VMEM((far, KV, 2, D), f32),
        pltpu.VMEM((far, KV, 2, D), f32),
        pltpu.VMEM((KV, NG, D), f32),
        pltpu.VMEM((KV, NG, D), f32),
        pltpu.VMEM((KV, NG, D), f32),
        pltpu.VMEM((KV, NG, D), bf16),
        pltpu.VMEM((one, KV, NG, D), bf16),
        pltpu.VMEM((one, KV, NG, D), bf16),
        pltpu.VMEM((one, KV, NG, D), bf16),
        dma((one,)), dma((one,)),
        dma((two, NA)), dma((two, NA)),
        dma((two, NA)), dma((two, NA)),
        dma((one, KV)), dma((one, KV)),
        dma((far, KV)), dma((far, KV)),
        dma((far, KV)), dma((far, KV)),
        dma((far, KV)), dma((far, KV)),
        dma((one, KV)), dma((one, KV)),
        dma((one, KV)), dma((one, KV)),
    ]
    smem = pl.BlockSpec(memory_space=pltpu.SMEM)
    vmem = pl.BlockSpec(memory_space=pltpu.VMEM)
    anywhere = pl.BlockSpec(memory_space=pl.ANY)
    return pl.pallas_call(
        functools.partial(body, (NS, NA, NH, R, T, KV, G, S)),
        out_shape=(
            jax.ShapeDtypeStruct(hidden.shape, bf16),
            jax.ShapeDtypeStruct(hidden.shape, bf16),
        ),
        in_specs=[smem, smem, vmem, vmem] + [anywhere] * 9,
        out_specs=(vmem, vmem),
        scratch_shapes=scratch,
        compiler_params=pltpu.CompilerParams(collective_id=0, has_side_effects=True),
        name="decode",
    )(
        suffix_length,
        row_adapter_index,
        jnp.asarray(cos),
        jnp.asarray(sin),
        hidden,
        base_query_rows,
        fresh_key_value,
        suffix_key_value,
        prompt_key_value,
        query_down_factors,
        query_up_factors,
        output_down_factors,
        output_up_factors,
    )


def solution(mesh):
    rows = P(("groups", "seq", "adapter"), None, "head")
    caches = P(None, ("groups", "seq", "adapter"), None, "head")
    factors = P(("groups", "adapter"), None, "head")
    placed = (
        rows,
        rows,
        caches,
        caches,
        P(("groups", "seq", "adapter")),
        P(("groups", "seq", "adapter"), None),
        P(None, ("groups", "seq"), "head"),
        factors,
        factors,
        factors,
        factors,
    )
    return jax.shard_map(
        on_device, mesh=mesh, in_specs=placed, out_specs=(rows, rows), check_vma=False
    )
```

time: 159 us -> 55.2 us (0.35)
  waiting for transfers between devices: 51.2 us -> 0 us
  Pallas kernels: 0 us -> 45 us
  blocking collectives: 38.6 us -> 0 us
  between operations: 15.8 us -> 0.64 us
  starting transfers between devices: 13.3 us -> 0 us
  local copies, waits for them, and re-layouts: 21.6 us -> 9.21 us
  matrix products: 10.3 us -> 0 us
  other arithmetic: 7.28 us -> 0 us
    pallas_call x0 -> x1, Pallas kernels: none -> 45 us  [on_device(): pl.pallas_call(functools.partial(body, (NS, NA, NH, R, T, KV, G, S)), out...]
    unnamed x4 -> x0, waiting for transfers between devices: 38.2 us -> none
    all_gather x3 -> x0, blocking collectives: 26.8 us -> none  [the longest x1 15.5 us: on_device(): gathered = lax.all_gather(query_flat, 'seq', axis=0, tiled=True)]
    all_to_all x3 -> x0, starting transfers between devices: 13.2 us -> none  [the longest x1 5.38 us: on_device(): lax.all_to_all(totals, 'seq', split_axis=0, concat_axis=0, tiled=True)]
    all_to_all x3 -> x0, waiting for transfers between devices: 13.1 us -> none  [the longest x1 8.4 us: on_device(): lax.all_to_all(weighted, 'seq', split_axis=0, concat_axis=0, tiled=True)]
    dot_general x8 -> x0, matrix products: 10.3 us -> none  [the longest x1 4.01 us: prompt_block(): jnp.einsum('nkgp,pkd->nkgd', weight, prompt_values, preferred_element_typ...]
    psum x2 -> x0, blocking collectives: 6.59 us -> none  [the longest x1 3.29 us: on_device(): out_whole = lax.psum(output_piece, 'head').astype(jnp.bfloat16)]
    unnamed x37 -> x4, local copies, waits for them, and re-layouts: 12.4 us -> 5.93 us
  transfers between devices with their start and end apart: 5 -> 0, of which waited for: 5 -> 0; matrix products, arithmetic and copies ran while one was open for 14% -> 0% of each run, Pallas kernels for 0% -> 0%
where the time goes in v1:
time: 55.2 us; the launch traced here: 54.8 us
  Pallas kernels  45 us (82%)
  local copies, waits for them, and re-layouts  9.21 us (17%)
  between operations  0.64 us (1%)
    pallas_call x1, Pallas kernels, on_device(): pl.pallas_call(functools.partial(body, (NS, NA, NH, R, T, KV, G, S)), out...  45 us
    unnamed x4, local copies, waits for them, and re-layouts  5.93 us
    pallas_call x2, local copies, waits for them, and re-layouts, on_device(): pl.pallas_call(functools.partial(body, (NS, NA, NH, R, T, KV, G, S)), out...  3.28 us

profile of v1, /device:TPU:0, one launch (start us, length us, event | category | flops | bytes accessed | tf_op | source)
XLA Modules:
  0.0 54.8 jit_solution(11252847521312832229)
XLA Ops:
  0.6 1.3 %copy.15.id_ref = s32[4,1]{1,0:T(4,128)} copy(s32[4,1]{0,1:T(1,128)} %param.18) | data formatting | bytes 32 | tf_op args[5]
  1.9 1.4 %copy.18.fresh_hbm = bf16[2,4,3,512]{3,2,1,0:T(4,128)(2,1)} copy(bf16[2,4,3,512]{3,1,2,0:T(4,128)(2,1)} %param.15) | data formatting | bytes 49152 | tf_op args[2]
  3.3 1.6 %copy.16.hidden_hbm = bf16[4,3,4096]{2,1,0:T(4,128)(2,1)} copy(bf16[4,3,4096]{2,0,1:T(4,128)(2,1)} %param.13) | data formatting | bytes 196608 | tf_op args[0]
  4.9 1.6 %copy.17.base_hbm = bf16[4,3,4096]{2,1,0:T(4,128)(2,1)} copy(bf16[4,3,4096]{2,0,1:T(4,128)(2,1)} %param.14) | data formatting | bytes 196608 | tf_op args[1]
  6.6 45.0 %decode.1 = (bf16[4,3,4096]{2,1,0:T(4,128)(2,1)}, bf16[4,3,4096]{2,1,0:T(4,128)(2,1)}) custom-call(s32[4]{0:T(128)} %len_ref.1, s32[4,1]{1,0:T(4,128)} %copy.15.id_ref, f32[35,128]{1,0:T(8,128)} %constant.4.clone.cos_ref, f32[35,128]{1,0:T(8,128)} %constant.5.clone.sin_ref, bf16[4,3,4096]{2,1,0:T(4,128)(2,1)} %copy.16.hidden_hbm, ...), custom_call_target="tpu_custom_call" | custom-call | tf_op jit(solution)/shard_map/decode/pallas_call | solution.py:511
  51.5 1.6 %copy.19 = bf16[4,3,4096]{2,0,1:T(4,128)(2,1)} copy(bf16[4,3,4096]{2,1,0:T(4,128)(2,1)} %get-tuple-element.2) | data formatting | bytes 196608 | tf_op jit(solution)/shard_map/decode/pallas_call | solution.py:511
  53.2 1.6 %copy.20 = bf16[4,3,4096]{2,0,1:T(4,128)(2,1)} copy(bf16[4,3,4096]{2,1,0:T(4,128)(2,1)} %get-tuple-element.3) | data formatting | bytes 196608 | tf_op jit(solution)/shard_map/decode/pallas_call | solution.py:511

commit v2 on v1

--- a/solution.py
+++ b/solution.py
@@ -157,8 +157,8 @@
         )
 
     def gather_tokens(ref):
-        for r in range(R):
-            tok_f32[r * T : (r + 1) * T, :] = ref[r].astype(jnp.float32)
+        for t in range(T):
+            tok_f32[t * R : (t + 1) * R, :] = ref[t].astype(jnp.float32)
         return tok_f32[...].astype(jnp.bfloat16)
 
     rk = {}
@@ -199,17 +199,17 @@
 
     def put_out(ref, x, k):
         rows_f32[...] = x
-        for r in range(R):
-            ref[r, :, k * C : (k + 1) * C] = jnp.concatenate(
-                [rows_f32[pl.ds(r * T * G + g, T, stride=G), :] for g in range(G)], 1
+        for t in range(T):
+            ref[t, :, k * C : (k + 1) * C] = jnp.concatenate(
+                [rows_f32[pl.ds(t * R * G + g, R, stride=G), :] for g in range(G)], 1
             ).astype(jnp.bfloat16)
 
     l_fresh.wait()
     fresh_pad[...] = jnp.zeros_like(fresh_pad)
     for i in range(2):
         fresh_f32[...] = jnp.zeros_like(fresh_f32)
-        for r in range(R):
-            fresh_f32[r * T : (r + 1) * T, :] = fresh_v[i, r].astype(jnp.float32)
+        for t in range(T):
+            fresh_f32[t * R : (t + 1) * R, :] = fresh_v[i, t].astype(jnp.float32)
         fresh_pad[i, 0 : fresh_f32.shape[0], :] = fresh_f32[...].astype(jnp.bfloat16)
 
     l_qu.wait()
@@ -227,13 +227,13 @@
     row_of = lax.broadcasted_iota(jnp.int32, (NG, D), 0)
     lane = lax.broadcasted_iota(jnp.int32, (NG, D), 1)
     eye = row_of == lane
-    row_index = row_of // (T * G)
+    step_of = row_of // (R * G)
+    row_index = row_of // G - step_of * R
     ids = jnp.zeros((NG, D), jnp.int32)
     lengths = jnp.zeros((NG, D), jnp.int32)
     for r in range(R):
-        ids = jnp.where(row_index == r, id_ref[r, 0], ids)
+        ids = jnp.where(row_index == r, id_ref[0, r], ids)
         lengths = jnp.where(row_index == r, len_ref[r], lengths)
-    step_of = (row_of - row_index * (T * G)) // G
 
     def pick(own, ref, k):
         out = own
@@ -244,10 +244,10 @@
         return out
 
     cos = jnp.concatenate(
-        [jnp.broadcast_to(cos_ref[pl.ds(len_ref[n // T] + n % T, 1), :], (G, D)) for n in range(N)], 0
+        [jnp.broadcast_to(cos_ref[pl.ds(len_ref[n % R] + n // R, 1), :], (G, D)) for n in range(N)], 0
     )
     sin = jnp.concatenate(
-        [jnp.broadcast_to(sin_ref[pl.ds(len_ref[n // T] + n % T, 1), :], (G, D)) for n in range(N)], 0
+        [jnp.broadcast_to(sin_ref[pl.ds(len_ref[n % R] + n // R, 1), :], (G, D)) for n in range(N)], 0
     )
 
     rank = rank_whole(0, rk_out, rk_in)
@@ -256,10 +256,10 @@
     order = sorted(range(1, NS), key=lambda d: (min(d, NS - d), d))
     for k in range(KV):
         delta = to_rows(dot_nn(rank, qu_v[0, :, k * C : (k + 1) * C]))
-        for r in range(R):
-            x = base_v[r, :, k * C : (k + 1) * C].astype(jnp.float32)
+        for t in range(T):
+            x = base_v[t, :, k * C : (k + 1) * C].astype(jnp.float32)
             for g in range(G):
-                rows_f32[pl.ds(r * T * G + g, T, stride=G), :] = x[:, g * D : (g + 1) * D]
+                rows_f32[pl.ds(t * R * G + g, R, stride=G), :] = x[:, g * D : (g + 1) * D]
         base = rows_f32[...]
         for d in range(1, NA):
             dl[(d, k)].wait_recv()
@@ -303,12 +303,11 @@
         return both[:, :D], peak, both[:, D:]
 
     n_suf = R * S
-    s_row = lax.broadcasted_iota(jnp.int32, (NG, n_suf), 0) // (T * G)
+    s_row = lax.broadcasted_iota(jnp.int32, (NG, n_suf), 0) // G % R
     s_col = lax.broadcasted_iota(jnp.int32, (NG, n_suf), 1)
     s_len = jnp.concatenate([lengths] * (n_suf // D), 1)
     in_suffix = (s_col // S == s_row) & (s_col - s_row * S < s_len)
-    f_slot = lane - row_index * T
-    in_fresh = (f_slot >= 0) & (f_slot <= step_of)
+    in_fresh = (lane % R == row_index) & (lane // R <= step_of)
     admitted = jnp.concatenate(
         [in_suffix.astype(jnp.int32), in_fresh.astype(jnp.int32)], 1
     ) != 0
@@ -421,6 +420,11 @@
 
     for copy in sends:
         copy.wait_send()
+
+
+def finish(first, second, att_ref, ada_ref):
+    att_ref[...] = first[...]
+    ada_ref[...] = second[...]
 
 
 def on_device(
@@ -437,7 +441,9 @@
     output_up_factors,
 ):
     NS, NA, NH = lax.axis_size("seq"), lax.axis_size("adapter"), lax.axis_size("head")
-    R, T, width = hidden.shape
+    hidden, base_query_rows = (x.transpose(1, 0, 2) for x in (hidden, base_query_rows))
+    fresh_key_value = fresh_key_value.transpose(0, 2, 1, 3)
+    T, R, width = hidden.shape
     D = HEAD_SIZE
     KV = prompt_key_value.shape[2] // D
     G = width // D // KV
@@ -508,7 +514,7 @@
     smem = pl.BlockSpec(memory_space=pltpu.SMEM)
     vmem = pl.BlockSpec(memory_space=pltpu.VMEM)
     anywhere = pl.BlockSpec(memory_space=pl.ANY)
-    return pl.pallas_call(
+    results = pl.pallas_call(
         functools.partial(body, (NS, NA, NH, R, T, KV, G, S)),
         out_shape=(
             jax.ShapeDtypeStruct(hidden.shape, bf16),
@@ -521,7 +527,7 @@
         name="decode",
     )(
         suffix_length,
-        row_adapter_index,
+        row_adapter_index.transpose(1, 0),
         jnp.asarray(cos),
         jnp.asarray(sin),
         hidden,
@@ -534,6 +540,14 @@
         output_down_factors,
         output_up_factors,
     )
+    results = pl.pallas_call(
+        finish,
+        out_shape=tuple(jax.ShapeDtypeStruct(x.shape, bf16) for x in results),
+        in_specs=[vmem, vmem],
+        out_specs=(vmem, vmem),
+        name="finish",
+    )(*results)
+    return tuple(x.transpose(1, 0, 2) for x in results)
 
 
 def solution(mesh):

time: 55.2 us -> 46.8 us (0.85)
  local copies, waits for them, and re-layouts: 9.21 us -> 0 us
  Pallas kernels: 45 us -> 45.9 us
    unnamed x4 -> x0, local copies, waits for them, and re-layouts: 5.93 us -> none
    pallas_call x2 -> x0, local copies, waits for them, and re-layouts: 3.28 us -> none  [on_device(): pl.pallas_call(functools.partial(body, (NS, NA, NH, R, T, KV, G, S)), out...]
    pallas_call x0 -> x1, Pallas kernels: none -> 1.62 us  [on_device(): pl.pallas_call(finish, out_shape=tuple((jax.ShapeDtypeStruct(x.shape, bf1...]
    pallas_call x1, Pallas kernels: 45 us -> 44.3 us  [on_device(): pl.pallas_call(functools.partial(body, (NS, NA, NH, R, T, KV, G, S)), out...]
where the time goes in v2:
time: 46.8 us; the launch traced here: 46.6 us
  Pallas kernels  45.9 us (98%)
  between operations  0.64 us (1%)
    pallas_call x1, Pallas kernels, on_device(): pl.pallas_call(functools.partial(body, (NS, NA, NH, R, T, KV, G, S)), out...  44.3 us
    pallas_call x1, Pallas kernels, on_device(): pl.pallas_call(finish, out_shape=tuple((jax.ShapeDtypeStruct(x.shape, bf1...  1.62 us

profile of v2, /device:TPU:0, one launch (start us, length us, event | category | flops | bytes accessed | tf_op | source)
XLA Modules:
  0.0 46.6 jit_solution(3785708679952093102)
XLA Ops:
  0.6 44.3 %decode.1 = (bf16[3,4,4096]{2,1,0:T(4,128)(2,1)}, bf16[3,4,4096]{2,1,0:T(4,128)(2,1)}) custom-call(s32[4]{0:T(128)} %len_ref.1, s32[1,4]{1,0:T(1,128)} %bitcast.9, f32[35,128]{1,0:T(8,128)} %constant.4.clone.cos_ref, f32[35,128]{1,0:T(8,128)} %constant.5.clone.sin_ref, bf16[3,4,4096]{2,1,0:T(4,128)(2,1)} %bitcast.6, bf16[3,4,4096]{2,1,0:T(4,128)(2,1)} %bitcast.7, ...), custom_call_target="tpu_custom_call" | custom-call | tf_op jit(solution)/shard_map/decode/pallas_call | solution.py:517
  45.0 1.6 %finish.1 = (bf16[3,4,4096]{2,1,0:T(4,128)(2,1)}, bf16[3,4,4096]{2,1,0:T(4,128)(2,1)}) custom-call(bf16[3,4,4096]{2,1,0:T(4,128)(2,1)} %get-tuple-element.6.first, bf16[3,4,4096]{2,1,0:T(4,128)(2,1)} %get-tuple-element.7.second), custom_call_target="tpu_custom_call" | custom-call | tf_op jit(solution)/shard_map/finish/pallas_call | solution.py:543
